TPU v7x, 32 devices: a whole 2x2x4 slice. The times are simulated.
32 devices in a mesh: mem: 4 (over z), lat: 8 (over y, x, core).
Axes of the slice: x: 2, y: 2, z: 4, core: 2. Of those that a mesh axis runs over, the one named last changes fastest.
Arguments:
- features: bfloat16 [16, 16, 1440, 128], P('mem', 'lat'), may hold values from -6 to 6
- conv_inner: bfloat16 [3, 3, 128, 128], replicated, may hold values from -0.1875 to 0.1875
- conv_head: bfloat16 [3, 3, 128, 69], replicated, may hold values from -0.1875 to 0.1875
- truth: float32 [69, 16, 1440], P(None, 'lat'), may hold values from -5 to 5
- kernel_width: float32 [69], replicated, may hold values from 0.3 to 1.5
- var_weight: float32 [69], replicated, may hold values from 0.5 to 2
Outputs:
- grad_features: bfloat16 [16, 16, 1440, 128], P('mem', 'lat')
- grad_inner: float32 [3, 3, 128, 128], replicated
- grad_head: float32 [3, 3, 128, 69], replicated
All inputs are finite; a program needn't handle non-finite values.
Results may differ from a plain program's by a relative error of at most 0.0098.
Values may be sent and summed in bfloat16 or wider, within the bound.
No kernel may reach another device: no remote copies, remote signals or barrier semaphores. Data moves between devices by JAX's collectives and lax.ppermute only.
A program may use at most 256 MiB of HBM per device.

v0:
```python
import jax
import jax.numpy as jnp
from jax import lax
from jax.sharding import PartitionSpec as P


def padded_2(cells, sides, width):
    for axis, dim in sides:
        count = lax.axis_size(axis)
        ends = count - 1
        head = lax.slice_in_dim(cells, 0, width, axis=dim)
        tail = lax.slice_in_dim(cells, cells.shape[dim] - width, cells.shape[dim], axis=dim)
        cells = jnp.concatenate(
            [
                lax.ppermute(tail, axis, [(i, (i + 1) % count) for i in range(ends)]),
                cells,
                lax.ppermute(head, axis, [((i + 1) % count, i) for i in range(ends)]),
            ],
            axis=dim,
        )
    return cells


def wrap_lon(values, axis):
    count = values.shape[axis]
    return jnp.concatenate(
        [
            lax.slice_in_dim(values, count - 1, count, axis=axis),
            values,
            lax.slice_in_dim(values, 0, 1, axis=axis),
        ],
        axis=axis,
    )


def gelu_slope(pre):
    return jax.jvp(jax.nn.gelu, (pre,), (jnp.ones_like(pre),))[1]


def hidden_conv(padded, kernel, band_rows):
    lon_cells = padded.shape[2] - 2
    summed = jnp.zeros((padded.shape[0], band_rows, lon_cells, kernel.shape[3]), jnp.float32)
    for row_off in range(3):
        for col_off in range(3):
            summed = summed + jnp.einsum(
                "mrlc,co->mrlo",
                padded[:, row_off : row_off + band_rows, col_off : col_off + lon_cells],
                kernel[row_off, col_off],
                preferred_element_type=jnp.float32,
            )
    return summed


def field_conv(padded, kernel, band_rows):
    lon_cells = padded.shape[2] - 2
    summed = jnp.zeros((padded.shape[0], kernel.shape[3], band_rows, lon_cells), jnp.float32)
    for row_off in range(3):
        for col_off in range(3):
            summed = summed + jnp.einsum(
                "mrlc,cv->mvrl",
                padded[:, row_off : row_off + band_rows, col_off : col_off + lon_cells],
                kernel[row_off, col_off],
                preferred_element_type=jnp.float32,
            )
    return summed


def field_back(padded_grad, kernel, band_rows):
    lon_cells = padded_grad.shape[3] - 2
    summed = jnp.zeros((padded_grad.shape[0], band_rows, lon_cells, kernel.shape[2]), jnp.float32)
    for row_off in range(3):
        for col_off in range(3):
            summed = summed + jnp.einsum(
                "mvrl,cv->mrlc",
                padded_grad[
                    :,
                    :,
                    2 - row_off : 2 - row_off + band_rows,
                    2 - col_off : 2 - col_off + lon_cells,
                ],
                kernel[row_off, col_off],
                preferred_element_type=jnp.float32,
            )
    return summed


def hidden_back(padded_grad, kernel, band_rows):
    lon_cells = padded_grad.shape[2] - 2
    summed = jnp.zeros((padded_grad.shape[0], band_rows, lon_cells, kernel.shape[2]), jnp.float32)
    for row_off in range(3):
        for col_off in range(3):
            summed = summed + jnp.einsum(
                "mrlo,co->mrlc",
                padded_grad[
                    :, 2 - row_off : 2 - row_off + band_rows, 2 - col_off : 2 - col_off + lon_cells
                ],
                kernel[row_off, col_off],
                preferred_element_type=jnp.float32,
            )
    return summed


def kernel_grad(padded_input, grad_out, form, band_rows, lon_cells):
    pieces = []
    for row_off in range(3):
        for col_off in range(3):
            pieces.append(
                jnp.einsum(
                    form,
                    padded_input[:, row_off : row_off + band_rows, col_off : col_off + lon_cells],
                    grad_out,
                    preferred_element_type=jnp.float32,
                )
            )
    return jnp.stack(pieces).reshape((3, 3) + pieces[0].shape)


def pair_sums(own, others, inverse):
    spread = others[None] - own[:, None]
    kernel = jnp.exp(-0.5 * spread * spread * inverse[None, None, :, None, None])
    return jnp.sum(kernel * spread, axis=1)


def member_grad(own, pairwise, truth_piece, inverse, var_weight, members):
    offset = own - truth_piece[None]
    nearness = jnp.exp(-0.5 * offset * offset * inverse[None, :, None, None])
    scale = (var_weight * inverse)[None, :, None, None]
    return scale * (2.0 / (members - 1) * pairwise + 2.0 * nearness * offset)


def split_groups(values, blocks, group):
    shaped = values.reshape((values.shape[0], blocks, group) + values.shape[2:])
    return jnp.moveaxis(shaped, 1, 0)


def shards(features, conv_inner, conv_head, truth, kernel_width, var_weight):
    band_rows = features.shape[1]
    lon_cells = features.shape[2]
    variables = conv_head.shape[3]
    feature_ext = padded_2(features, (("lat", 1),), 1)
    pre_own = hidden_conv(wrap_lon(feature_ext, 2), conv_inner, band_rows)
    hidden_own = jax.nn.gelu(pre_own).astype(jnp.bfloat16)
    hidden_ext = padded_2(hidden_own, (("lat", 1),), 1)
    hidden_wrap = wrap_lon(hidden_ext, 2)
    field = field_conv(hidden_wrap, conv_head, band_rows).astype(jnp.bfloat16)
    inverse = 1.0 / (kernel_width * kernel_width)
    group = 3
    blocks = variables // group
    inverse_blocks = inverse.reshape(blocks, group)
    gathered = lax.all_to_all(field, "mem", split_axis=3, concat_axis=0, tiled=True)
    values = gathered.astype(jnp.float32)
    members = values.shape[0]
    piece_cells = values.shape[3]

    def block_pairs(packed):
        member_values, rates = packed
        return pair_sums(member_values, member_values, rates)

    pairwise = lax.map(block_pairs, (split_groups(values, blocks, group), inverse_blocks))
    pairwise = jnp.moveaxis(pairwise, 0, 1).reshape(values.shape)
    truth_piece = lax.dynamic_slice_in_dim(
        truth, lax.axis_index("mem") * piece_cells, piece_cells, 2
    )
    gradient = member_grad(values, pairwise, truth_piece, inverse, var_weight, members).astype(
        jnp.bfloat16
    )
    field_grad = lax.all_to_all(gradient, "mem", split_axis=0, concat_axis=3, tiled=True)
    grad_pad = padded_2(field_grad, (("lat", 2),), 1)
    hidden_grad = (
        field_back(wrap_lon(grad_pad, 3), conv_head, band_rows) * gelu_slope(pre_own)
    ).astype(jnp.bfloat16)
    head_grad = kernel_grad(hidden_wrap, field_grad, "mrlc,mvrl->cv", band_rows, lon_cells)
    hidden_pad = padded_2(hidden_grad, (("lat", 1),), 1)
    grad_features = hidden_back(wrap_lon(hidden_pad, 2), conv_inner, band_rows).astype(jnp.bfloat16)
    inner_grad = kernel_grad(
        wrap_lon(feature_ext, 2), hidden_grad, "mrlc,mrlo->co", band_rows, lon_cells
    )
    inner_sum, head_sum = lax.psum((inner_grad, head_grad), ("mem", "lat"))
    points = band_rows * lax.axis_size("lat") * lon_cells
    return (grad_features, inner_sum / points, head_sum / points)


def solution(mesh):
    in_specs = (P("mem", "lat", None, None), P(), P(), P(None, "lat", None), P(), P())
    out_specs = (P("mem", "lat", None, None), P(), P())
    return jax.shard_map(shards, mesh=mesh, in_specs=in_specs, out_specs=out_specs, check_vma=False)
```

profile of v0, /device:TPU:0, one launch (start us, length us, event | category | flops | bytes accessed | tf_op | source)
XLA Modules:
  0.0 686.2 jit_solution(3638382335253527599)
XLA Ops:
  13.2 3.5 fusion.177
  19.7 4.1 fusion.183
  23.7 4.0 fusion.173
  31.1 3.4 fusion.163
  34.5 3.4 fusion.180
  44.7 21.2 %multiply_convert_fusion = (bf16[4,2,1440,128]{3,2,1,0:T(8,128)(2,1)}, f32[4,2,1440,128]{3,2,1,0:T(8,128)}) fusion(bf16[3,3,128,128]{3,2,1,0:T(8,128)(2,1)S(1)} %copy-done.21, bf16[4,4,1,128]{3,2,1,0:T(2,128)(2,1)S(1)} %get-tuple-element.58, bf16[4,4,1440,128]{3,2,1,0:T(8,128)(2,1)} %copy-done.2, f32[4,2,1440,128]{3,2,1,0:T(8,128)} %fusion.168, ...), kind=kOutput, calls=%fused_computation.41 | convolution fusion | flops 408453120 | bytes 61972480 | tf_op jit(solution)/shard_map/mrlc,co->mrlo/dot_general | solution.py:45
  68.1 30.4 %collective-permute-start.2 = (bf16[4,1,1440,128]{3,2,1,0:T(8,128)(2,1)S(1)}, bf16[4,1,1440,128]{3,2,1,0:T(8,128)(2,1)S(1)}, u32[]{:S(2)}, u32[]{:S(2)}) collective-permute-start(bf16[4,1,1440,128]{3,2,1,0:T(8,128)(2,1)S(1)} %get-tuple-element.64), channel_id=1, source_target_pairs={{0,1},{1,2},{2,3},{3,4},{4,5},{5,6},{6,7},{8,9},{9,10},{10,11},{11... | collective-permute-start | bytes 4423688 | tf_op jit(solution)/shard_map/ppermute | solution.py:15
  103.7 7.3 %fusion.7 = (bf16[4,4,1441,128]{3,2,1,0:T(8,128)(2,1)S(1)}, bf16[4,4,1441,128]{3,2,1,0:T(8,128)(2,1)S(1)}) fusion(bf16[4,1,1440,128]{3,2,1,0:T(8,128)(2,1)S(1)} %collective-permute-done.3, bf16[4,2,1440,128]{3,2,1,0:T(8,128)(2,1)S(1)} %copy-done.5, bf16[4,1,1440,128]{3,2,1,0:T(8,128)(2,1)S(1)} %collective-permute-done.2), kind=kLoop, calls=%fused_computation.26 | loop fusion | flops 70828032 | bytes 17702912 | tf_op jit(solution)/shard_map/concatenate | solution.py:26
  111.0 4.1 fusion.76
  115.1 3.6 fusion.84
  118.7 3.6 fusion.92
  122.3 3.6 fusion.80
  126.0 3.6 fusion.88
  133.2 8.2 %fusion.71 = bf16[4,69,2,1440]{3,1,2,0:T(8,128)(2,1)} fusion(bf16[4,4,1441,128]{3,2,1,0:T(8,128)(2,1)S(1)} %get-tuple-element.57, f32[4,2,1440,69]{2,3,1,0:T(8,128)S(1)} %fusion.53, f32[4,2,1440,69]{2,3,1,0:T(8,128)} %fusion.76, f32[4,2,1440,69]{2,3,1,0:T(8,128)} %fusion.80, f32[4,2,1440,69]{2,3,1,0:T(8,128)S(1)} %fusion.218, ...), kind=kOutput, calls=%fused_computation.109 | convolution fusion | flops 210643200 | bytes 32868864 | tf_op jit(solution)/shard_map/mrlc,cv->mvrl/dot_general | solution.py:59
  141.4 8.4 %copy.54 = bf16[4,69,2,1440]{1,2,0,3:T(2,128)(2,1)} copy(bf16[4,69,2,1440]{3,1,2,0:T(8,128)(2,1)} %fusion.71) | data formatting | bytes 3179520 | tf_op jit(solution)/shard_map/convert_element_type | solution.py:145
  149.8 4.9 all-to-all-start
  155.2 46.0 %all-to-all-done = bf16[4,69,2,1440]{1,2,0,3:T(2,128)(2,1)} async-done(((bf16[4,69,2,1440]{1,2,0,3:T(2,128)(2,1)}), bf16[4,69,2,1440]{1,2,0,3:T(2,128)(2,1)}, u32[]{:S(2)}, u32[]{:S(2)}) %all-to-all-start) | async-done | bytes 1589792 | tf_op jit(solution)/shard_map/all_to_all | solution.py:150
  201.1 7.7 %copy.55 = bf16[4,69,2,1440]{3,0,2,1:T(4,128)(2,1)S(1)} copy(bf16[4,69,2,1440]{1,2,0,3:T(2,128)(2,1)} %all-to-all-done) | data formatting | bytes 3179520 | tf_op jit(solution)/shard_map/all_to_all | solution.py:150
  208.9 3.8 reshape.78
  212.7 5.6 copy.57
  218.3 3.7 copy.60
  222.1 61.3 %while.10 = (s32[]{:T(128)}, f32[23,16,3,2,360]{4,1,3,2,0:T(8,128)}, f32[23,16,3,2,360]{4,3,2,0,1:T(2,128)}, f32[23,3]{1,0:T(8,128)S(1)}, s32[]{:T(128)}) while((s32[]{:T(128)}, f32[23,16,3,2,360]{4,1,3,2,0:T(8,128)}, f32[23,16,3,2,360]{4,3,2,0,1:T(2,128)}, f32[23,3]{1,0:T(8,128)S(1)}, s32[]{:T(128)}) %tuple.48), condition=%wide.region_2.3_spmd, body=%wide.region_0.2_spmd.sunk | while | flops 3283202 | bytes 1253493 | solution.py:159
  291.0 25.7 %all_to_all.27 = bf16[16,69,2,360]{3,2,1,0:T(2,128)(2,1)S(1)} all-to-all(bf16[16,69,2,360]{3,2,1,0:T(2,128)(2,1)S(1)} %copy.62), channel_id=1, replica_groups=mesh['mem'=4,'lat'=8] {'mem'}, dimensions={0} | all-to-all | bytes 3179520 | tf_op jit(solution)/shard_map/all_to_all | solution.py:167
  319.5 3.5 all_to_all.24
  334.7 22.2 %collective-permute-start.4 = (bf16[4,69,1,1440]{3,0,2,1:T(4,128)(2,1)S(1)}, bf16[4,69,1,1440]{3,0,2,1:T(4,128)(2,1)S(1)}, u32[]{:S(2)}, u32[]{:S(2)}) collective-permute-start(bf16[4,69,1,1440]{3,0,2,1:T(4,128)(2,1)S(1)} %copy.65), channel_id=1, source_target_pairs={{0,1},{1,2},{2,3},{3,4},{4,5},{5,6},{6,7},{8,9},{9,10},{10,11},{11... | collective-permute-start | bytes 2384648 | tf_op jit(solution)/shard_map/ppermute | solution.py:15
  360.5 3.5 fusion.216
  364.4 43.1 %collective-permute-done.5 = bf16[4,69,1,1440]{3,0,2,1:T(4,128)(2,1)S(1)} collective-permute-done((bf16[4,69,1,1440]{3,0,2,1:T(4,128)(2,1)S(1)}, bf16[4,69,1,1440]{3,0,2,1:T(4,128)(2,1)S(1)}, u32[]{:S(2)}, u32[]{:S(2)}) %collective-permute-start.5) | collective-permute-done | bytes 794912 | tf_op jit(solution)/shard_map/ppermute | solution.py:17
  407.8 4.2 fusion.98
  412.0 4.2 fusion.95
  416.3 4.1 fusion.104
  420.4 4.1 fusion.108
  424.5 4.2 fusion.101
  428.6 4.0 fusion.57
  432.6 3.6 fusion.61
  436.2 21.4 %fusion.19 = bf16[4,2,1440,128]{3,2,1,0:T(8,128)(2,1)} fusion(f32[4,2,1440,128]{3,2,1,0:T(8,128)} %get-tuple-element.82, f32[4,2,1440,128]{3,2,1,0:T(8,128)} %fusion.61, f32[4,2,1440,128]{3,2,1,0:T(8,128)} %fusion.108, f32[4,2,1440,128]{3,2,1,0:T(8,128)} %fusion.95, f32[4,2,1440,128]{3,2,1,0:T(8,128)} %fusion.216, f32[4,2,1440,128]{3,2,1,0:T(8,128)} %fusion.101, ...), kind=kOutput, calls=%fused_computation.39 | convolution fusion | flops 245007360 | bytes 59526144 | tf_op jit(solution)/shard_map/mvrl,cv->mrlc/dot_general | solution.py:73
  457.6 3.9 fusion.118
  473.5 17.4 %collective-permute-start.6 = (bf16[4,1,1440,128]{3,2,1,0:T(8,128)(2,1)}, bf16[4,1,1440,128]{3,2,1,0:T(8,128)(2,1)}, u32[]{:S(2)}, u32[]{:S(2)}) collective-permute-start(bf16[4,1,1440,128]{3,2,1,0:T(8,128)(2,1)} %get-tuple-element.63), channel_id=1, source_target_pairs={{0,1},{1,2},{2,3},{3,4},{4,5},{5,6},{6,7},{8,9},{9,10},{10,11},{11... | collective-permute-start | bytes 4423688 | tf_op jit(solution)/shard_map/ppermute | solution.py:15
  493.8 5.2 fusion.175
  499.1 122.8 %all-reduce.3.cloned.1.call-done = (f32[3,3,128,128]{3,2,1,0:T(8,128)}, f32[3,3,128,69]{2,3,1,0:T(8,128)}) async-done(((f32[3,3,128,128]{3,2,1,0:T(8,128)}, f32[3,3,128,69]{2,3,1,0:T(8,128)}), (f32[3,3,128,128]{3,2,1,0:T(8,128)}, f32[3,3,128,69]{2,3,1,0:T(8,128)})) %all-reduce.3.cloned.1.call-update) | async-done | bytes 907792 | tf_op jit(solution)/shard_map/psum | solution.py:178
  625.5 7.7 %fusion.4 = (bf16[4,4,1441,128]{3,2,1,0:T(8,128)(2,1)S(1)}, bf16[4,4,1441,128]{3,2,1,0:T(8,128)(2,1)S(1)}) fusion(bf16[4,1,1440,128]{3,2,1,0:T(8,128)(2,1)S(1)} %collective-permute-done.7, bf16[4,2,1440,128]{3,2,1,0:T(8,128)(2,1)} %fusion.19, bf16[4,1,1440,128]{3,2,1,0:T(8,128)(2,1)} %collective-permute-done.6), kind=kLoop, calls=%fused_computation.17 | loop fusion | flops 70828032 | bytes 17702912 | tf_op jit(solution)/shard_map/concatenate | solution.py:26
  633.2 3.9 fusion.45
  637.5 3.5 fusion.49
  641.0 3.6 fusion.43
  644.6 3.5 fusion.47
  648.0 3.5 fusion.51
  651.5 4.8 fusion.24
  656.3 3.5 fusion.20
  659.8 19.4 %add_convert_fusion = bf16[4,2,1440,128]{3,2,1,0:T(8,128)(2,1)} fusion(f32[4,2,1440,128]{3,2,1,0:T(8,128)} %fusion.24, f32[4,2,1440,128]{3,2,1,0:T(8,128)} %fusion.43, f32[4,2,1440,128]{3,2,1,0:T(8,128)} %fusion.45, f32[4,2,1440,128]{3,2,1,0:T(8,128)} %fusion.175, f32[4,2,1440,128]{3,2,1,0:T(8,128)} %fusion.47, f32[4,2,1440,128]{3,2,1,0:T(8,128)} %fusion.49, ...), kind=kOutput, calls=%fused_computation.40 | convolution fusion | flops 390758400 | bytes 53116928 | tf_op jit(solution)/shard_map/mrlo,co->mrlc/dot_general | solution.py:92
  (253 shorter events, 136.5 us)
Async XLA Ops:
  7.2 147.7 %copy-start = (f32[69,2,1440]{2,1,0:T(2,128)S(1)}, f32[69,2,1440]{2,1,0:T(2,128)}, u32[]{:S(2)}) copy-start(f32[69,2,1440]{2,1,0:T(2,128)} %param.11) | copy-start | bytes 2384644
  7.2 6.0 copy-start.9
  7.2 6.0 copy-start.21
  9.4 7.3 %collective-permute-start = (bf16[4,1,1440,128]{3,2,1,0:T(8,128)(2,1)S(1)}, bf16[4,1,1440,128]{3,2,1,0:T(8,128)(2,1)S(1)}, u32[]{:S(2)}, u32[]{:S(2)}) collective-permute-start(bf16[4,1,1440,128]{3,2,1,0:T(8,128)(2,1)S(1)} %get-tuple-element.69), channel_id=1, source_target_pairs={{0,1},{1,2},{2,3},{3,4},{4,5},{5,6},{6,7},{8,9},{9,10},{10,11},{11... | collective-permute-start | bytes 4423688 | tf_op jit(solution)/shard_map/ppermute | solution.py:15
  11.9 7.2 %collective-permute-start.1 = (bf16[4,1,1440,128]{3,2,1,0:T(8,128)(2,1)S(1)}, bf16[4,1,1440,128]{3,2,1,0:T(8,128)(2,1)S(1)}, u32[]{:S(2)}, u32[]{:S(2)}) collective-permute-start(bf16[4,1,1440,128]{3,2,1,0:T(8,128)(2,1)S(1)} %get-tuple-element.70), channel_id=1, source_target_pairs={{1,0},{2,1},{3,2},{4,3},{5,4},{6,5},{7,6},{9,8},{10,9},{11,10},{12... | collective-permute-start | bytes 4423688 | tf_op jit(solution)/shard_map/ppermute | solution.py:17
  19.0 22.4 %copy-start.15 = (bf16[4,3,1440,128]{3,2,1,0:T(8,128)(2,1)}, bf16[4,3,1440,128]{3,2,1,0:T(8,128)(2,1)S(1)}, u32[]{:S(2)}) copy-start(bf16[4,3,1440,128]{3,2,1,0:T(8,128)(2,1)S(1)} %get-tuple-element.66) | copy-start | bytes 13271044
  19.6 14.9 %copy-start.2 = (bf16[4,4,1440,128]{3,2,1,0:T(8,128)(2,1)}, bf16[4,4,1440,128]{3,2,1,0:T(8,128)(2,1)S(1)}, u32[]{:S(2)}) copy-start(bf16[4,4,1440,128]{3,2,1,0:T(8,128)(2,1)S(1)} %get-tuple-element.75) | copy-start | bytes 17694724
  19.6 18.3 %copy-start.13 = (bf16[4,3,1440,128]{3,2,1,0:T(8,128)(2,1)}, bf16[4,3,1440,128]{3,2,1,0:T(8,128)(2,1)S(1)}, u32[]{:S(2)}) copy-start(bf16[4,3,1440,128]{3,2,1,0:T(8,128)(2,1)S(1)} %get-tuple-element.76) | copy-start | bytes 13271044
  66.0 34.1 %copy-start.5 = (bf16[4,2,1440,128]{3,2,1,0:T(8,128)(2,1)S(1)}, bf16[4,2,1440,128]{3,2,1,0:T(8,128)(2,1)}, u32[]{:S(2)}) copy-start(bf16[4,2,1440,128]{3,2,1,0:T(8,128)(2,1)} %get-tuple-element.81) | copy-start | bytes 8847364
  66.0 34.1 %copy-start.22 = (bf16[3,3,128,69]{2,3,1,0:T(8,128)(2,1)S(1)}, bf16[3,3,128,69]{2,3,1,0:T(8,128)(2,1)}, u32[]{:S(2)}) copy-start(bf16[3,3,128,69]{2,3,1,0:T(8,128)(2,1)} %param.10) | copy-start | bytes 476932
  68.1 33.7 %collective-permute-start.2 = (bf16[4,1,1440,128]{3,2,1,0:T(8,128)(2,1)S(1)}, bf16[4,1,1440,128]{3,2,1,0:T(8,128)(2,1)S(1)}, u32[]{:S(2)}, u32[]{:S(2)}) collective-permute-start(bf16[4,1,1440,128]{3,2,1,0:T(8,128)(2,1)S(1)} %get-tuple-element.64), channel_id=1, source_target_pairs={{0,1},{1,2},{2,3},{3,4},{4,5},{5,6},{6,7},{8,9},{9,10},{10,11},{11... | collective-permute-start | bytes 4423688 | tf_op jit(solution)/shard_map/ppermute | solution.py:15
  98.5 5.2 collective-permute-start.3
  101.9 29.5 %copy-start.19 = (bf16[4,1,1440,128]{3,2,1,0:T(8,128)(2,1)}, bf16[4,1,1440,128]{3,2,1,0:T(8,128)(2,1)S(1)}, u32[]{:S(2)}) copy-start(bf16[4,1,1440,128]{3,2,1,0:T(8,128)(2,1)S(1)} %collective-permute-done.2) | copy-start | bytes 4423684
  103.7 25.8 %copy-start.17 = (bf16[4,1,1440,128]{3,2,1,0:T(8,128)(2,1)}, bf16[4,1,1440,128]{3,2,1,0:T(8,128)(2,1)S(1)}, u32[]{:S(2)}) copy-start(bf16[4,1,1440,128]{3,2,1,0:T(8,128)(2,1)S(1)} %collective-permute-done.3) | copy-start | bytes 4423684
  111.0 7.7 %copy-start.12 = (bf16[4,4,1441,128]{3,2,1,0:T(8,128)(2,1)}, bf16[4,4,1441,128]{3,2,1,0:T(8,128)(2,1)S(1)}, u32[]{:S(2)}) copy-start(bf16[4,4,1441,128]{3,2,1,0:T(8,128)(2,1)S(1)} %get-tuple-element.56) | copy-start | bytes 17707012
  111.0 22.2 %copy-start.11 = (bf16[4,4,1441,128]{3,2,1,0:T(8,128)(2,1)}, bf16[4,4,1441,128]{3,2,1,0:T(8,128)(2,1)S(1)}, u32[]{:S(2)}) copy-start(bf16[4,4,1441,128]{3,2,1,0:T(8,128)(2,1)S(1)} %get-tuple-element.57) | copy-start | bytes 17707012
  141.4 13.4 %copy-start.26 = (f32[69]{0:T(128)S(1)}, f32[69]{0:T(128)}, u32[]{:S(2)}) copy-start(f32[69]{0:T(128)} %param.13) | copy-start | bytes 832
  141.4 13.4 %copy-start.27 = (f32[69]{0:T(128)S(1)}, f32[69]{0:T(128)}, u32[]{:S(2)}) copy-start(f32[69]{0:T(128)} %param.12) | copy-start | bytes 832
  149.8 51.3 %all-to-all-start = ((bf16[4,69,2,1440]{1,2,0,3:T(2,128)(2,1)}), bf16[4,69,2,1440]{1,2,0,3:T(2,128)(2,1)}, u32[]{:S(2)}, u32[]{:S(2)}) async-start(bf16[4,69,2,1440]{1,2,0,3:T(2,128)(2,1)} %copy.54), calls=%async_computation | async-start | bytes 5898240 | tf_op jit(solution)/shard_map/all_to_all | solution.py:150
  154.7 467.1 %all-reduce.3.cloned.1.call-start = ((), (), s32[]{:S(2)}) async-start(), calls=%async_computation.2 | async-start | bytes 1843200 | tf_op jit(solution)/shard_map/psum | solution.py:178
  212.7 5.6 copy-start.14
  283.4 3.0 copy-start.16
  323.0 2.9 copy-start.6
  323.0 3.1 copy-start.20
  325.7 2.3 slice-start.2
  326.1 2.3 slice-start.3
  326.1 3.7 slice-start.4
  328.4 1.9 slice-start.5
  333.1 25.3 %copy-start.18 = (bf16[4,1,1440,128]{3,2,1,0:T(8,128)(2,1)S(1)}, bf16[4,1,1440,128]{3,2,1,0:T(8,128)(2,1)}, u32[]{:S(2)}) copy-start(bf16[4,1,1440,128]{3,2,1,0:T(8,128)(2,1)} %copy-done.17) | copy-start | bytes 4423684
  334.7 29.3 %collective-permute-start.4 = (bf16[4,69,1,1440]{3,0,2,1:T(4,128)(2,1)S(1)}, bf16[4,69,1,1440]{3,0,2,1:T(4,128)(2,1)S(1)}, u32[]{:S(2)}, u32[]{:S(2)}) collective-permute-start(bf16[4,69,1,1440]{3,0,2,1:T(4,128)(2,1)S(1)} %copy.65), channel_id=1, source_target_pairs={{0,1},{1,2},{2,3},{3,4},{4,5},{5,6},{6,7},{8,9},{9,10},{10,11},{11... | collective-permute-start | bytes 2384648 | tf_op jit(solution)/shard_map/ppermute | solution.py:15
  356.9 50.5 %collective-permute-start.5 = (bf16[4,69,1,1440]{3,0,2,1:T(4,128)(2,1)S(1)}, bf16[4,69,1,1440]{3,0,2,1:T(4,128)(2,1)S(1)}, u32[]{:S(2)}, u32[]{:S(2)}) collective-permute-start(bf16[4,69,1,1440]{3,0,2,1:T(4,128)(2,1)S(1)} %copy.66), channel_id=1, source_target_pairs={{1,0},{2,1},{3,2},{4,3},{5,4},{6,5},{7,6},{9,8},{10,9},{11,10},{12... | collective-permute-start | bytes 2384648 | tf_op jit(solution)/shard_map/ppermute | solution.py:17
  359.1 1.4 copy-start.23
  360.5 3.7 copy-start.25
  407.6 16.8 %copy-start.7 = (bf16[4,69,4,1440]{3,1,2,0:T(8,128)(2,1)}, bf16[4,69,4,1440]{3,1,2,0:T(8,128)(2,1)S(1)}, u32[]{:S(2)}) copy-start(bf16[4,69,4,1440]{3,1,2,0:T(8,128)(2,1)S(1)} %get-tuple-element.78) | copy-start | bytes 9538564
  457.6 4.0 copy-start.3
  457.6 8.6 %slice-start = ((s8[5898240]{0:T(1024)(128)(4,1)}), s8[4194304]{0:T(1024)(128)(4,1)S(1)}, s32[]{:S(2)}) async-start(s8[5898240]{0:T(1024)(128)(4,1)} %bitcast.371), calls=%async_computation.3 | async-start | bytes 8388608
  461.6 4.6 slice-start.1
  467.2 1.8 copy-start.10
  469.1 21.9 %slice-start.6 = ((s8[4423680]{0:T(1024)(128)(4,1)}), s8[4194304]{0:T(1024)(128)(4,1)S(1)}, s32[]{:S(2)}) async-start(s8[4423680]{0:T(1024)(128)(4,1)} %bitcast.377), calls=%async_computation.9 | async-start | bytes 8388608
  470.1 20.8 %slice-start.7 = ((s8[4423680]{0:T(1024)(128)(4,1)}), s8[229376]{0:T(1024)(128)(4,1)S(1)}, s32[]{:S(2)}) async-start(s8[4423680]{0:T(1024)(128)(4,1)} %bitcast.377), calls=%async_computation.10 | async-start | bytes 458752
  472.2 153.3 %collective-permute-start.7 = (bf16[4,1,1440,128]{3,2,1,0:T(8,128)(2,1)}, bf16[4,1,1440,128]{3,2,1,0:T(8,128)(2,1)S(1)}, u32[]{:S(2)}, u32[]{:S(2)}) collective-permute-start(bf16[4,1,1440,128]{3,2,1,0:T(8,128)(2,1)} %get-tuple-element.62), channel_id=1, source_target_pairs={{1,0},{2,1},{3,2},{4,3},{5,4},{6,5},{7,6},{9,8},{10,9},{11,10},{12... | collective-permute-start | bytes 4423688 | tf_op jit(solution)/shard_map/ppermute | solution.py:17
  473.5 152.0 %collective-permute-start.6 = (bf16[4,1,1440,128]{3,2,1,0:T(8,128)(2,1)}, bf16[4,1,1440,128]{3,2,1,0:T(8,128)(2,1)}, u32[]{:S(2)}, u32[]{:S(2)}) collective-permute-start(bf16[4,1,1440,128]{3,2,1,0:T(8,128)(2,1)} %get-tuple-element.63), channel_id=1, source_target_pairs={{0,1},{1,2},{2,3},{3,4},{4,5},{5,6},{6,7},{8,9},{9,10},{10,11},{11... | collective-permute-start | bytes 4423688 | tf_op jit(solution)/shard_map/ppermute | solution.py:15
  493.0 0.8 copy-start.24
  633.2 4.3 copy-start.8
  648.0 3.5 copy-start.4
  659.8 19.4 %copy-start.1 = (f32[69,2,1440]{2,1,0:T(2,128)S(1)}, f32[69,2,1440]{2,1,0:T(2,128)}, u32[]{:S(2)}) copy-start(f32[69,2,1440]{2,1,0:T(2,128)} %param.11) | copy-start | bytes 2384644
Sparse Core Ops, SparseCore 0:
  494.0 127.8 all-reduce.2
where the time goes:
time: 697 us; the launch traced here: 686 us
  waiting for transfers between devices  214 us (31%)
  matrix products  210 us (30%)
  local copies, waits for them, and re-layouts  90.5 us (13%)
  starting transfers between devices  82.9 us (12%)
  other arithmetic  47.9 us (7%)
  blocking collectives  25.7 us (4%)
  between operations  14.9 us (2%)
    psum x1, waiting for transfers between devices, shards(): inner_sum, head_sum = lax.psum((inner_grad, head_grad), ('mem', 'lat'))  123 us
    ppermute x4, starting transfers between devices, padded_2(): lax.ppermute(tail, axis, [(i, (i + 1) % count) for i in range(ends)])  72.5 us
    dot_general x9, matrix products, field_back(): jnp.einsum('mvrl,cv->mrlc', padded_grad[:, :, 2 - row_off:2 - row_off + b...  53.3 us
    dot_general x9, matrix products, hidden_back(): jnp.einsum('mrlo,co->mrlc', padded_grad[:, 2 - row_off:2 - row_off + band...  50.8 us
    dot_general x9, matrix products, hidden_conv(): jnp.einsum('mrlc,co->mrlo', padded[:, row_off:row_off + band_rows, col_of...  49.8 us
    all_to_all x1, waiting for transfers between devices, shards(): lax.all_to_all(field, 'mem', split_axis=3, concat_axis=0, tiled=True)  46 us
    ppermute x4, waiting for transfers between devices, padded_2(): lax.ppermute(head, axis, [((i + 1) % count, i) for i in range(ends)])  44.9 us
    dot_general x9, matrix products, field_conv(): jnp.einsum('mrlc,cv->mvrl', padded[:, row_off:row_off + band_rows, col_of...  32.1 us
  transfers between devices with their start and end apart: 10, of which 4 were waited for; matrix products, arithmetic and copies ran while one was open for 4% of the time, Pallas kernels for 0%

commit v1 on v0

--- a/solution.py
+++ b/solution.py
@@ -2,6 +2,20 @@
 import jax.numpy as jnp
 from jax import lax
 from jax.sharding import PartitionSpec as P
+
+
+def treat_the_ratios(x_local, ndim_at, my_data):
+    local_part, long_array = (x_local.shape[:ndim_at], x_local.shape[ndim_at + 1 :])
+    v_next = x_local.reshape(*local_part, my_data, -1, *long_array)
+    all_rows = jnp.moveaxis(v_next, ndim_at, 0)
+    return all_rows
+
+
+def derive_matrix(load, axis_no):
+    w1 = list(load.shape[1:])
+    w1[axis_no] *= load.shape[0]
+    b_now = jnp.moveaxis(load, 0, axis_no).reshape(w1)
+    return b_now
 
 
 def padded_2(cells, sides, width):
@@ -147,7 +161,19 @@
     group = 3
     blocks = variables // group
     inverse_blocks = inverse.reshape(blocks, group)
-    gathered = lax.all_to_all(field, "mem", split_axis=3, concat_axis=0, tiled=True)
+    view_out = jax.lax.axis_index("mem")
+    piece_out = jax.lax.axis_size("mem")
+    res, z1 = (piece_out, view_out)
+    clean = treat_the_ratios(field, 3, res)
+    d = 1
+    rack = [clean[z1]]
+    while d < res:
+        prior = clean[(z1 + d) % res]
+        y = jax.lax.ppermute(prior, axis_name="mem", perm=[(p, (p + d) % res) for p in range(res)])
+        rack.append(y)
+        d += 1
+    clean = jnp.stack(rack)[(z1 - jnp.arange(res)) % res]
+    gathered = derive_matrix(clean, 0)
     values = gathered.astype(jnp.float32)
     members = values.shape[0]
     piece_cells = values.shape[3]

time: 697 us -> 665 us (0.954)
  waiting for transfers between devices: 214 us -> 167 us
  local copies, waits for them, and re-layouts: 90.5 us -> 76.6 us
  starting transfers between devices: 82.9 us -> 91.3 us
  matrix products: 210 us -> 218 us
  other arithmetic: 47.9 us -> 55.1 us
    all_to_all x1 -> x0, waiting for transfers between devices: 46 us -> none  [shards(): lax.all_to_all(field, 'mem', split_axis=3, concat_axis=0, tiled=True)]
    ppermute x4, waiting for transfers between devices: 44.9 us -> 31.5 us  [padded_2(): lax.ppermute(head, axis, [((i + 1) % count, i) for i in range(ends)])]
    ppermute x0 -> x3, waiting for transfers between devices: none -> 13.2 us  [shards(): jax.lax.ppermute(prior, axis_name='mem', perm=[(p, (p + d) % res) for p i...]
    transpose x3 -> x1, local copies, waits for them, and re-layouts: 13.2 us -> 3.07 us  [split_groups(): return jnp.moveaxis(shaped, 1, 0)]
    convert_element_type x1 -> x0, local copies, waits for them, and re-layouts: 8.43 us -> none  [shards(): field = field_conv(hidden_wrap, conv_head, band_rows).astype(jnp.bfloat16)]
    all_to_all x1 -> x0, local copies, waits for them, and re-layouts: 7.72 us -> none  [shards(): lax.all_to_all(field, 'mem', split_axis=3, concat_axis=0, tiled=True)]
    ppermute x4, starting transfers between devices: 72.5 us -> 80.2 us  [padded_2(): lax.ppermute(tail, axis, [(i, (i + 1) % count) for i in range(ends)])]
  transfers between devices with their start and end apart: 10 -> 12, of which waited for: 4 -> 6; matrix products, arithmetic and copies ran while one was open for 4% -> 4% of each run, Pallas kernels for 0% -> 0%
where the time goes in v1:
time: 665 us; the launch traced here: 654 us
  matrix products  218 us (33%)
  waiting for transfers between devices  167 us (25%)
  starting transfers between devices  91.3 us (14%)
  local copies, waits for them, and re-layouts  76.6 us (12%)
  other arithmetic  55.1 us (8%)
  blocking collectives  30.5 us (5%)
  between operations  15.2 us (2%)
    psum x1, waiting for transfers between devices, shards(): inner_sum, head_sum = lax.psum((inner_grad, head_grad), ('mem', 'lat'))  123 us
    ppermute x4, starting transfers between devices, padded_2(): lax.ppermute(tail, axis, [(i, (i + 1) % count) for i in range(ends)])  80.2 us
    dot_general x9, matrix products, field_back(): jnp.einsum('mvrl,cv->mrlc', padded_grad[:, :, 2 - row_off:2 - row_off + b...  53.1 us
    dot_general x9, matrix products, hidden_back(): jnp.einsum('mrlo,co->mrlc', padded_grad[:, 2 - row_off:2 - row_off + band...  50.8 us
    dot_general x9, matrix products, hidden_conv(): jnp.einsum('mrlc,co->mrlo', padded[:, row_off:row_off + band_rows, col_of...  49.8 us
    dot_general x9, matrix products, field_conv(): jnp.einsum('mrlc,cv->mvrl', padded[:, row_off:row_off + band_rows, col_of...  37.3 us
    ppermute x4, waiting for transfers between devices, padded_2(): lax.ppermute(head, axis, [((i + 1) % count, i) for i in range(ends)])  31.5 us
    all_to_all x1, blocking collectives, shards(): lax.all_to_all(gradient, 'mem', split_axis=0, concat_axis=3, tiled=True)  30.5 us
  transfers between devices with their start and end apart: 12, of which 6 were waited for; matrix products, arithmetic and copies ran while one was open for 4% of the time, Pallas kernels for 0%

profile of v1, /device:TPU:0, one launch (start us, length us, event | category | flops | bytes accessed | tf_op | source)
XLA Modules:
  0.0 654.5 jit_solution(16913464918550817654)
XLA Ops:
  13.2 3.5 fusion.177
  19.7 4.1 fusion.183
  23.8 4.0 fusion.173
  31.2 3.4 fusion.163
  34.6 3.4 fusion.180
  38.0 3.4 fusion.168
  44.8 21.2 %multiply_convert_fusion = (bf16[4,2,1440,128]{3,2,1,0:T(8,128)(2,1)}, f32[4,2,1440,128]{3,2,1,0:T(8,128)}) fusion(bf16[3,3,128,128]{3,2,1,0:T(8,128)(2,1)S(1)} %copy-done.16, bf16[4,4,1,128]{3,2,1,0:T(2,128)(2,1)S(1)} %get-tuple-element.54, bf16[4,4,1440,128]{3,2,1,0:T(8,128)(2,1)} %copy-done.2, f32[4,2,1440,128]{3,2,1,0:T(8,128)} %fusion.168, ...), kind=kOutput, calls=%fused_computation.42 | convolution fusion | flops 408453120 | bytes 61972480 | tf_op jit(solution)/shard_map/mrlc,co->mrlo/dot_general | solution.py:59
  66.1 3.7 fusion.276
  69.8 31.7 %collective-permute-start.2 = (bf16[4,1,1440,128]{3,2,1,0:T(8,128)(2,1)}, bf16[4,1,1440,128]{3,2,1,0:T(8,128)(2,1)}, u32[]{:S(2)}, u32[]{:S(2)}) collective-permute-start(bf16[4,1,1440,128]{3,2,1,0:T(8,128)(2,1)} %get-tuple-element.60), channel_id=1, source_target_pairs={{0,1},{1,2},{2,3},{3,4},{4,5},{5,6},{6,7},{8,9},{9,10},{10,11},{11... | collective-permute-start | bytes 4423688 | tf_op jit(solution)/shard_map/ppermute | solution.py:29
  102.9 3.8 fusion.218
  107.1 9.6 %fusion.7 = (bf16[4,4,1441,128]{3,2,1,0:T(8,128)(2,1)S(1)}, bf16[4,4,1441,128]{3,2,1,0:T(8,128)(2,1)S(1)}) fusion(bf16[4,1,1440,128]{3,2,1,0:T(8,128)(2,1)} %collective-permute-done.3, bf16[4,2,1440,128]{3,2,1,0:T(8,128)(2,1)S(1)} %copy-done.5, bf16[4,1,1440,128]{3,2,1,0:T(8,128)(2,1)} %collective-permute-done.2), kind=kLoop, calls=%fused_computation.27 | loop fusion | flops 70828032 | bytes 17702912 | tf_op jit(solution)/shard_map/concatenate | solution.py:40
  116.7 4.1 fusion.76
  120.7 3.7 fusion.84
  124.4 3.6 fusion.92
  128.0 3.6 fusion.80
  131.7 3.6 fusion.88
  141.6 8.5 %fusion.71 = bf16[4,69,2,1440]{3,1,2,0:T(8,128)(2,1)} fusion(bf16[4,4,1441,128]{3,2,1,0:T(8,128)(2,1)S(1)} %get-tuple-element.53, f32[4,2,1440,69]{2,3,1,0:T(8,128)S(1)} %fusion.53, f32[4,2,1440,69]{2,3,1,0:T(8,128)} %fusion.76, f32[4,2,1440,69]{2,3,1,0:T(8,128)} %fusion.80, f32[4,2,1440,69]{2,3,1,0:T(8,128)S(1)} %fusion.218, ...), kind=kOutput, calls=%fused_computation.110 | convolution fusion | flops 210643200 | bytes 31071744 | tf_op jit(solution)/shard_map/mrlc,cv->mvrl/dot_general | solution.py:73
  150.1 4.2 reshape.91
  154.4 3.6 constant_dynamic-slice_fusion.5
  165.6 3.8 collective-permute-done.4
  169.4 9.4 %collective-permute-done.5 = bf16[4,69,2,360]{3,1,2,0:T(8,128)(2,1)} collective-permute-done((bf16[4,69,2,360]{3,1,2,0:T(8,128)(2,1)S(1)}, bf16[4,69,2,360]{3,1,2,0:T(8,128)(2,1)}, u32[]{:S(2)}, u32[]{:S(2)}) %collective-permute-start.5) | collective-permute-done | bytes 397472 | tf_op jit(solution)/shard_map/ppermute | solution.py:172
  189.3 61.3 %while.10 = (s32[]{:T(128)}, f32[23,16,3,2,360]{4,1,3,2,0:T(8,128)}, f32[23,16,3,2,360]{4,3,2,0,1:T(2,128)}, f32[23,3]{1,0:T(8,128)S(1)}, s32[]{:T(128)}) while((s32[]{:T(128)}, f32[23,16,3,2,360]{4,1,3,2,0:T(8,128)}, f32[23,16,3,2,360]{4,3,2,0,1:T(2,128)}, f32[23,3]{1,0:T(8,128)S(1)}, s32[]{:T(128)}) %tuple.50), condition=%wide.region_2.3_spmd, body=%wide.region_0.2_spmd.sunk | while | flops 3283202 | bytes 1253493 | solution.py:185
  258.2 30.5 %all_to_all.18 = bf16[16,69,2,360]{3,2,1,0:T(2,128)(2,1)S(1)} all-to-all(bf16[16,69,2,360]{3,2,1,0:T(2,128)(2,1)S(1)} %copy.37), channel_id=1, replica_groups=mesh['mem'=4,'lat'=8] {'mem'}, dimensions={0} | all-to-all | bytes 3179520 | tf_op jit(solution)/shard_map/all_to_all | solution.py:193
  291.5 3.5 all_to_all.16
  307.2 28.5 %collective-permute-start.7 = (bf16[4,69,1,1440]{3,0,2,1:T(4,128)(2,1)S(1)}, bf16[4,69,1,1440]{3,0,2,1:T(4,128)(2,1)S(1)}, u32[]{:S(2)}, u32[]{:S(2)}) collective-permute-start(bf16[4,69,1,1440]{3,0,2,1:T(4,128)(2,1)S(1)} %copy.40), channel_id=1, source_target_pairs={{0,1},{1,2},{2,3},{3,4},{4,5},{5,6},{6,7},{8,9},{9,10},{10,11},{11... | collective-permute-start | bytes 2384648 | tf_op jit(solution)/shard_map/ppermute | solution.py:29
  340.8 3.5 fusion.216
  344.7 31.0 %collective-permute-done.8 = bf16[4,69,1,1440]{3,0,2,1:T(4,128)(2,1)S(1)} collective-permute-done((bf16[4,69,1,1440]{3,0,2,1:T(4,128)(2,1)S(1)}, bf16[4,69,1,1440]{3,0,2,1:T(4,128)(2,1)S(1)}, u32[]{:S(2)}, u32[]{:S(2)}) %collective-permute-start.8) | collective-permute-done | bytes 794912 | tf_op jit(solution)/shard_map/ppermute | solution.py:31
  376.1 4.2 fusion.98
  380.4 4.3 fusion.95
  384.6 4.1 fusion.104
  388.7 4.1 fusion.108
  392.8 4.2 fusion.101
  397.0 3.7 fusion.57
  400.7 3.6 fusion.61
  404.3 21.4 %fusion.19 = bf16[4,2,1440,128]{3,2,1,0:T(8,128)(2,1)} fusion(f32[4,2,1440,128]{3,2,1,0:T(8,128)} %get-tuple-element.82, f32[4,2,1440,128]{3,2,1,0:T(8,128)} %fusion.61, f32[4,2,1440,128]{3,2,1,0:T(8,128)} %fusion.108, f32[4,2,1440,128]{3,2,1,0:T(8,128)} %fusion.95, f32[4,2,1440,128]{3,2,1,0:T(8,128)} %fusion.216, f32[4,2,1440,128]{3,2,1,0:T(8,128)} %fusion.101, ...), kind=kOutput, calls=%fused_computation.40 | convolution fusion | flops 245007360 | bytes 59526144 | tf_op jit(solution)/shard_map/mvrl,cv->mrlc/dot_general | solution.py:87
  425.7 3.9 fusion.118
  441.6 17.5 %collective-permute-start.9 = (bf16[4,1,1440,128]{3,2,1,0:T(8,128)(2,1)}, bf16[4,1,1440,128]{3,2,1,0:T(8,128)(2,1)}, u32[]{:S(2)}, u32[]{:S(2)}) collective-permute-start(bf16[4,1,1440,128]{3,2,1,0:T(8,128)(2,1)} %get-tuple-element.59), channel_id=1, source_target_pairs={{0,1},{1,2},{2,3},{3,4},{4,5},{5,6},{6,7},{8,9},{9,10},{10,11},{11... | collective-permute-start | bytes 4423688 | tf_op jit(solution)/shard_map/ppermute | solution.py:29
  462.0 5.2 fusion.175
  467.2 122.7 %all-reduce.3.cloned.1.call-done = (f32[3,3,128,128]{3,2,1,0:T(8,128)}, f32[3,3,128,69]{2,3,1,0:T(8,128)}) async-done(((f32[3,3,128,128]{3,2,1,0:T(8,128)}, f32[3,3,128,69]{2,3,1,0:T(8,128)}), (f32[3,3,128,128]{3,2,1,0:T(8,128)}, f32[3,3,128,69]{2,3,1,0:T(8,128)})) %all-reduce.3.cloned.1.call-update) | async-done | bytes 907792 | tf_op jit(solution)/shard_map/psum | solution.py:204
  593.6 7.7 %fusion.4 = (bf16[4,4,1441,128]{3,2,1,0:T(8,128)(2,1)S(1)}, bf16[4,4,1441,128]{3,2,1,0:T(8,128)(2,1)S(1)}) fusion(bf16[4,1,1440,128]{3,2,1,0:T(8,128)(2,1)S(1)} %collective-permute-done.10, bf16[4,2,1440,128]{3,2,1,0:T(8,128)(2,1)} %fusion.19, bf16[4,1,1440,128]{3,2,1,0:T(8,128)(2,1)} %collective-permute-done.9), kind=kLoop, calls=%fused_computation.18 | loop fusion | flops 70828032 | bytes 17702912 | tf_op jit(solution)/shard_map/concatenate | solution.py:40
  601.3 3.9 fusion.45
  605.6 3.5 fusion.49
  609.1 3.6 fusion.43
  612.7 3.5 fusion.47
  616.1 3.5 fusion.51
  619.6 4.8 fusion.24
  624.4 3.5 fusion.20
  627.9 19.4 %add_convert_fusion = bf16[4,2,1440,128]{3,2,1,0:T(8,128)(2,1)} fusion(f32[4,2,1440,128]{3,2,1,0:T(8,128)} %fusion.24, f32[4,2,1440,128]{3,2,1,0:T(8,128)} %fusion.43, f32[4,2,1440,128]{3,2,1,0:T(8,128)} %fusion.45, f32[4,2,1440,128]{3,2,1,0:T(8,128)} %fusion.175, f32[4,2,1440,128]{3,2,1,0:T(8,128)} %fusion.47, f32[4,2,1440,128]{3,2,1,0:T(8,128)} %fusion.49, ...), kind=kOutput, calls=%fused_computation.41 | convolution fusion | flops 390758400 | bytes 53116928 | tf_op jit(solution)/shard_map/mrlo,co->mrlc/dot_general | solution.py:106
  (258 shorter events, 149.9 us)
Async XLA Ops:
  7.2 157.4 %copy-start = (f32[69,2,1440]{2,1,0:T(2,128)S(1)}, f32[69,2,1440]{2,1,0:T(2,128)}, u32[]{:S(2)}) copy-start(f32[69,2,1440]{2,1,0:T(2,128)} %param.11) | copy-start | bytes 2384644
  7.2 6.0 copy-start.16
  7.2 582.8 %all-reduce.3.cloned.1.call-start = ((), (), s32[]{:S(2)}) async-start(), calls=%async_computation.1 | async-start | bytes 1843200 | tf_op jit(solution)/shard_map/psum | solution.py:204
  7.2 6.0 copy-start.9
  9.4 7.3 %collective-permute-start = (bf16[4,1,1440,128]{3,2,1,0:T(8,128)(2,1)S(1)}, bf16[4,1,1440,128]{3,2,1,0:T(8,128)(2,1)S(1)}, u32[]{:S(2)}, u32[]{:S(2)}) collective-permute-start(bf16[4,1,1440,128]{3,2,1,0:T(8,128)(2,1)S(1)} %get-tuple-element.65), channel_id=1, source_target_pairs={{0,1},{1,2},{2,3},{3,4},{4,5},{5,6},{6,7},{8,9},{9,10},{10,11},{11... | collective-permute-start | bytes 4423688 | tf_op jit(solution)/shard_map/ppermute | solution.py:29
  11.9 7.2 %collective-permute-start.1 = (bf16[4,1,1440,128]{3,2,1,0:T(8,128)(2,1)S(1)}, bf16[4,1,1440,128]{3,2,1,0:T(8,128)(2,1)S(1)}, u32[]{:S(2)}, u32[]{:S(2)}) collective-permute-start(bf16[4,1,1440,128]{3,2,1,0:T(8,128)(2,1)S(1)} %get-tuple-element.66), channel_id=1, source_target_pairs={{1,0},{2,1},{3,2},{4,3},{5,4},{6,5},{7,6},{9,8},{10,9},{11,10},{12... | collective-permute-start | bytes 4423688 | tf_op jit(solution)/shard_map/ppermute | solution.py:31
  19.0 22.4 %copy-start.14 = (bf16[4,3,1440,128]{3,2,1,0:T(8,128)(2,1)}, bf16[4,3,1440,128]{3,2,1,0:T(8,128)(2,1)S(1)}, u32[]{:S(2)}) copy-start(bf16[4,3,1440,128]{3,2,1,0:T(8,128)(2,1)S(1)} %get-tuple-element.62) | copy-start | bytes 13271044
  19.7 15.0 %copy-start.2 = (bf16[4,4,1440,128]{3,2,1,0:T(8,128)(2,1)}, bf16[4,4,1440,128]{3,2,1,0:T(8,128)(2,1)S(1)}, u32[]{:S(2)}) copy-start(bf16[4,4,1440,128]{3,2,1,0:T(8,128)(2,1)S(1)} %get-tuple-element.75) | copy-start | bytes 17694724
  19.7 18.4 %copy-start.13 = (bf16[4,3,1440,128]{3,2,1,0:T(8,128)(2,1)}, bf16[4,3,1440,128]{3,2,1,0:T(8,128)(2,1)S(1)}, u32[]{:S(2)}) copy-start(bf16[4,3,1440,128]{3,2,1,0:T(8,128)(2,1)S(1)} %get-tuple-element.76) | copy-start | bytes 13271044
  66.1 36.8 %copy-start.19 = (bf16[3,3,128,69]{2,3,1,0:T(8,128)(2,1)S(1)}, bf16[3,3,128,69]{2,3,1,0:T(8,128)(2,1)}, u32[]{:S(2)}) copy-start(bf16[3,3,128,69]{2,3,1,0:T(8,128)(2,1)} %param.10) | copy-start | bytes 476932
  69.8 36.9 %collective-permute-start.2 = (bf16[4,1,1440,128]{3,2,1,0:T(8,128)(2,1)}, bf16[4,1,1440,128]{3,2,1,0:T(8,128)(2,1)}, u32[]{:S(2)}, u32[]{:S(2)}) collective-permute-start(bf16[4,1,1440,128]{3,2,1,0:T(8,128)(2,1)} %get-tuple-element.60), channel_id=1, source_target_pairs={{0,1},{1,2},{2,3},{3,4},{4,5},{5,6},{6,7},{8,9},{9,10},{10,11},{11... | collective-permute-start | bytes 4423688 | tf_op jit(solution)/shard_map/ppermute | solution.py:29
  101.6 5.5 collective-permute-start.3
  102.9 4.2 copy-start.5
  116.6 7.8 %copy-start.12 = (bf16[4,4,1441,128]{3,2,1,0:T(8,128)(2,1)}, bf16[4,4,1441,128]{3,2,1,0:T(8,128)(2,1)S(1)}, u32[]{:S(2)}) copy-start(bf16[4,4,1441,128]{3,2,1,0:T(8,128)(2,1)S(1)} %get-tuple-element.52) | copy-start | bytes 17707012
  116.6 25.0 %copy-start.11 = (bf16[4,4,1441,128]{3,2,1,0:T(8,128)(2,1)}, bf16[4,4,1441,128]{3,2,1,0:T(8,128)(2,1)S(1)}, u32[]{:S(2)}) copy-start(bf16[4,4,1441,128]{3,2,1,0:T(8,128)(2,1)S(1)} %get-tuple-element.53) | copy-start | bytes 17707012
  154.3 10.1 %copy-start.23 = (f32[69]{0:T(128)S(1)}, f32[69]{0:T(128)}, u32[]{:S(2)}) copy-start(f32[69]{0:T(128)} %param.13) | copy-start | bytes 832
  154.4 10.1 %copy-start.24 = (f32[69]{0:T(128)S(1)}, f32[69]{0:T(128)}, u32[]{:S(2)}) copy-start(f32[69]{0:T(128)} %param.12) | copy-start | bytes 832
  158.9 10.5 %collective-permute-start.4 = (bf16[4,69,2,360]{3,1,2,0:T(8,128)(2,1)}, bf16[4,69,2,360]{3,1,2,0:T(8,128)(2,1)S(1)}, u32[]{:S(2)}, u32[]{:S(2)}) collective-permute-start(bf16[4,69,2,360]{3,1,2,0:T(8,128)(2,1)} %bitcast.377), channel_id=1, source_target_pairs={{0,8},{8,16},{16,24},{24,0},{1,9},{9,17},{17,25},{25,1},{2,10},{10... | collective-permute-start | bytes 1192328 | tf_op jit(solution)/shard_map/ppermute | solution.py:172
  160.5 18.4 %collective-permute-start.5 = (bf16[4,69,2,360]{3,1,2,0:T(8,128)(2,1)S(1)}, bf16[4,69,2,360]{3,1,2,0:T(8,128)(2,1)}, u32[]{:S(2)}, u32[]{:S(2)}) collective-permute-start(bf16[4,69,2,360]{3,1,2,0:T(8,128)(2,1)S(1)} %bitcast.401), channel_id=1, source_target_pairs={{0,16},{8,24},{16,0},{24,8},{1,17},{9,25},{17,1},{25,9},{2,18},{10... | collective-permute-start | bytes 1192328 | tf_op jit(solution)/shard_map/ppermute | solution.py:172
  163.1 15.8 %collective-permute-start.6 = (bf16[4,69,2,360]{3,1,2,0:T(8,128)(2,1)S(1)}, bf16[4,69,2,360]{3,1,2,0:T(8,128)(2,1)}, u32[]{:S(2)}, u32[]{:S(2)}) collective-permute-start(bf16[4,69,2,360]{3,1,2,0:T(8,128)(2,1)S(1)} %bitcast.399), channel_id=1, source_target_pairs={{0,24},{8,0},{16,8},{24,16},{1,25},{9,1},{17,9},{25,17},{2,26},{10... | collective-permute-start | bytes 1192328 | tf_op jit(solution)/shard_map/ppermute | solution.py:172
  250.6 3.0 copy-start.15
  250.6 3.0 copy-start.18
  295.0 2.9 copy-start.6
  297.7 2.6 slice-start.2
  297.9 3.0 slice-start.3
  297.9 4.3 slice-start.4
  300.8 1.9 slice-start.5
  307.2 37.2 %collective-permute-start.7 = (bf16[4,69,1,1440]{3,0,2,1:T(4,128)(2,1)S(1)}, bf16[4,69,1,1440]{3,0,2,1:T(4,128)(2,1)S(1)}, u32[]{:S(2)}, u32[]{:S(2)}) collective-permute-start(bf16[4,69,1,1440]{3,0,2,1:T(4,128)(2,1)S(1)} %copy.40), channel_id=1, source_target_pairs={{0,1},{1,2},{2,3},{3,4},{4,5},{5,6},{6,7},{8,9},{9,10},{10,11},{11... | collective-permute-start | bytes 2384648 | tf_op jit(solution)/shard_map/ppermute | solution.py:29
  335.6 40.1 %collective-permute-start.8 = (bf16[4,69,1,1440]{3,0,2,1:T(4,128)(2,1)S(1)}, bf16[4,69,1,1440]{3,0,2,1:T(4,128)(2,1)S(1)}, u32[]{:S(2)}, u32[]{:S(2)}) collective-permute-start(bf16[4,69,1,1440]{3,0,2,1:T(4,128)(2,1)S(1)} %copy.41), channel_id=1, source_target_pairs={{1,0},{2,1},{3,2},{4,3},{5,4},{6,5},{7,6},{9,8},{10,9},{11,10},{12... | collective-permute-start | bytes 2384648 | tf_op jit(solution)/shard_map/ppermute | solution.py:31
  339.4 1.4 copy-start.20
  340.8 3.7 copy-start.22
  376.0 16.8 %copy-start.7 = (bf16[4,69,4,1440]{3,1,2,0:T(8,128)(2,1)}, bf16[4,69,4,1440]{3,1,2,0:T(8,128)(2,1)S(1)}, u32[]{:S(2)}) copy-start(bf16[4,69,4,1440]{3,1,2,0:T(8,128)(2,1)S(1)} %get-tuple-element.78) | copy-start | bytes 9538564
  425.7 3.9 copy-start.3
  425.7 8.5 %slice-start = ((s8[5898240]{0:T(1024)(128)(4,1)}), s8[4194304]{0:T(1024)(128)(4,1)S(1)}, s32[]{:S(2)}) async-start(s8[5898240]{0:T(1024)(128)(4,1)} %bitcast.385), calls=%async_computation.2 | async-start | bytes 8388608
  429.6 4.6 slice-start.1
  435.3 1.8 copy-start.10
  437.1 21.9 %slice-start.6 = ((s8[4423680]{0:T(1024)(128)(4,1)}), s8[4194304]{0:T(1024)(128)(4,1)S(1)}, s32[]{:S(2)}) async-start(s8[4423680]{0:T(1024)(128)(4,1)} %bitcast.391), calls=%async_computation.8 | async-start | bytes 8388608
  438.2 20.9 %slice-start.7 = ((s8[4423680]{0:T(1024)(128)(4,1)}), s8[229376]{0:T(1024)(128)(4,1)S(1)}, s32[]{:S(2)}) async-start(s8[4423680]{0:T(1024)(128)(4,1)} %bitcast.391), calls=%async_computation.9 | async-start | bytes 458752
  440.3 153.3 %collective-permute-start.10 = (bf16[4,1,1440,128]{3,2,1,0:T(8,128)(2,1)}, bf16[4,1,1440,128]{3,2,1,0:T(8,128)(2,1)S(1)}, u32[]{:S(2)}, u32[]{:S(2)}) collective-permute-start(bf16[4,1,1440,128]{3,2,1,0:T(8,128)(2,1)} %get-tuple-element.58), channel_id=1, source_target_pairs={{1,0},{2,1},{3,2},{4,3},{5,4},{6,5},{7,6},{9,8},{10,9},{11,10},{12... | collective-permute-start | bytes 4423688 | tf_op jit(solution)/shard_map/ppermute | solution.py:31
  441.6 152.0 %collective-permute-start.9 = (bf16[4,1,1440,128]{3,2,1,0:T(8,128)(2,1)}, bf16[4,1,1440,128]{3,2,1,0:T(8,128)(2,1)}, u32[]{:S(2)}, u32[]{:S(2)}) collective-permute-start(bf16[4,1,1440,128]{3,2,1,0:T(8,128)(2,1)} %get-tuple-element.59), channel_id=1, source_target_pairs={{0,1},{1,2},{2,3},{3,4},{4,5},{5,6},{6,7},{8,9},{9,10},{10,11},{11... | collective-permute-start | bytes 4423688 | tf_op jit(solution)/shard_map/ppermute | solution.py:29
  460.1 1.9 copy-start.17
  461.1 0.8 copy-start.21
  601.3 4.3 copy-start.8
  616.1 3.5 copy-start.4
  627.9 19.4 %copy-start.1 = (f32[69,2,1440]{2,1,0:T(2,128)S(1)}, f32[69,2,1440]{2,1,0:T(2,128)}, u32[]{:S(2)}) copy-start(f32[69,2,1440]{2,1,0:T(2,128)} %param.11) | copy-start | bytes 2384644
Sparse Core Ops, SparseCore 0:
  462.1 127.8 all-reduce.2
